TPU v7x, 128 devices: a whole 4x4x4 slice. The times are simulated.
128 devices in a mesh: dp: 4 (over x), tm: 32 (over z, y, core).
Axes of the slice: x: 4, y: 4, z: 4, core: 2. Of those that a mesh axis runs over, the one named last changes fastest.
Arguments:
- clips: bfloat16 [4, 512, 512, 512], P('dp', 'tm'), may hold values from -6 to 6
- w_time: bfloat16 [3, 512, 512], P(None, 'dp'), may hold values from -0.15625 to 0.15625
- gain: float32 [512], replicated, may hold values from 0.1 to 1.9
- rate: float32 [512], replicated, may hold values from 9.765625e-05 to 0.0333333333
- keep: float32 [512], P('tm'), may hold values from 0.5 to 1
- latent_ids: int32 [512], P('tm'), may hold values from 0 to 63, as said below
- w_lat: bfloat16 [512, 16], replicated, may hold values from -0.25 to 0.25
Outputs:
- features: bfloat16 [4, 512, 512, 512], P('dp', 'tm')
- latents: float32 [4, 64, 16, 512], P('dp', 'tm')
Inputs may be any that keep to these rules, and one draw needn't show every extreme that they name: latent_ids never falls as the frame grows; latent frame j begins at a frame from j * 8 - 7 to j * 8 (latent 0 at frame 0) and ends where the next begins; every latent frame gets 1 to 15 frames and the last exactly 15.
All inputs are finite; a program needn't handle non-finite values.
Results may differ from a plain program's by a relative error of at most 0.0025.
Values may be sent and summed in bfloat16 or wider, within the bound.
No kernel may reach another device: no remote copies, remote signals or barrier semaphores. Data moves between devices by JAX's collectives and lax.ppermute only.
A program may use at most 192 MiB of HBM per device.

v0:
```python
import functools

import jax
import jax.numpy as jnp
from jax import lax
from jax.experimental import pallas as pl
from jax.experimental.pallas import tpu as pltpu
from jax.sharding import PartitionSpec as P


KT = 3
STRIDE = 8
F32 = jnp.float32
BF16 = jnp.bfloat16
TILE = 128
GROUP = 4
ROWS = 256
SUB = 16


def rotated(value, axis, steps):
    count = lax.axis_size(axis)
    return lax.ppermute(value, axis, [(s, (s + steps) % count) for s in range(count)])


def shifted(value, axis, steps):
    count = lax.axis_size(axis)
    return lax.ppermute(value, axis, [(s, s + steps) for s in range(count - steps)])


def swapped(value, axis):
    return lax.ppermute(value, axis, [(s, s ^ 1) for s in range(lax.axis_size(axis))])


def pieces_of(value):
    one = value.astype(BF16).astype(F32)
    two = (value - one).astype(BF16).astype(F32)
    return one, two, value - one - two


def times(a, b):
    return lax.dot_general(a, b, (((1,), (1,)), ((), ())), preferred_element_type=F32)


def split(value):
    upper = value.astype(BF16)
    return upper, (value - upper.astype(F32)).astype(BF16)


def spread_kernel(packed, rate, constants, last, own, sends, counts, E):
    nall, lanes = packed.shape
    nchan = rate.shape[1]
    ndev, per, width = sends.shape
    nproj = own.shape[0] // 3
    nlat = ndev * per // nproj
    me = lax.axis_index("tm")
    end = (me + 1) * (nall // lax.axis_size("tm")) - 1
    frame = lax.broadcasted_iota(jnp.int32, (nall, lanes), 0)
    lane = lax.broadcasted_iota(jnp.int32, (nall, lanes), 1)
    logs = jnp.where(frame > end, jnp.log(packed[:, 0:1]), 0.0)
    one, two, three = pieces_of(logs)
    pieces = jnp.where(lane == 0, one, jnp.where(lane == 1, two, jnp.where(lane == 2, three, 0.0)))
    rows = lax.broadcasted_iota(jnp.int32, (nall, nall), 0)
    cols = lax.broadcasted_iota(jnp.int32, (nall, nall), 1)
    lower = jnp.where(cols <= rows, 1.0, 0.0).astype(BF16)
    run = jnp.dot(lower, pieces.astype(BF16), preferred_element_type=F32)
    run = jnp.sum(run, -1, keepdims=True)
    block = 128
    for r in range(0, nall, block):
        at = lax.broadcasted_iota(jnp.int32, (block, nchan), 0) + r
        gap = (at - end).astype(F32)
        E[r : r + block, :] = jnp.where(at > end, jnp.exp(run[r : r + block] - rate[...] * gap), 0.0)
    ids = packed[:, lanes // 2 : lanes // 2 + 1].astype(jnp.int32)
    member = jnp.where(lane == ids, 1.0, 0.0).astype(BF16)
    table = jnp.zeros((lanes, nchan), F32)
    for piece in pieces_of(E[...]):
        table = table + lax.dot_general(
            member, piece.astype(BF16), (((0,), (0,)), ((), ())), preferred_element_type=F32
        )
    for i in range(counts.shape[0]):
        hit = (jnp.broadcast_to(ids, (nall, lanes)) == me * counts.shape[0] + i).astype(F32)
        counts[i : i + 1, :] = jnp.sum(hit, 0, keepdims=True)
    E[0:lanes, :] = table
    scaled = constants[0:nproj, :]
    top, rest = split(last[...])
    rows = 256
    group = rows // nproj
    for r in range(0, nlat, group):
        value = jnp.concatenate([scaled * E[j : j + 1, :] for j in range(r, r + group)], 0)
        upper, lower = split(value)
        z = times(jnp.concatenate([upper, lower], 0), top)
        z = z[:rows] + z[rows:] + times(upper, rest)
        first = r * nproj // per
        sends[first : first + rows // per] = z.reshape(rows // per, per, width).astype(BF16)

    @pl.when(me < ndev - 1)
    def _():
        block = sends[me + 1]
        moved = own[2 * nproj : 3 * nproj, :]
        sends[me + 1, 0:nproj] = (block[0:nproj].astype(F32) + moved).astype(BF16)


def conv_kernel(
    window, packing, x_hbm, halo_hbm, mine, da, db, dc, so, sa, sb, sc, constants,
    feat_hbm, last, sums, w, X, HA, HB, FA, FB, R, pooled, kept, wsem, insem, outsem, *, shards,
):
    nframe, npos, nchan = x_hbm.shape
    tiles, groups = npos // TILE, nframe // GROUP
    total = tiles * groups
    H, F = (HA, HB), (FA, FB)
    half = da.shape[1]
    depth = 2 * half
    nproj = sums.shape[0] // 3
    me = lax.axis_index("dp")
    side = lax.rem(lax.axis_index("tm"), 2)
    lead = KT - 1

    def weights():
        copies = []
        slot = 0
        for step, near, far in ((0, mine, so), (shards - 1, da, sa), (1, db, sb), (2, dc, sc)):
            base = lax.rem(me + step, shards) * depth
            for piece, lane in ((near, side), (far, 1 - side)):
                row = pl.multiple_of(base + lane * half, half)
                copies.append(pltpu.make_async_copy(piece, w.at[:, pl.ds(row, half)], wsem.at[slot]))
                slot += 1
        return copies

    def entering(q):
        part = pl.ds(q * TILE, TILE)
        return pltpu.make_async_copy(x_hbm.at[:, part], X.at[lead : lead + nframe, part], insem.at[q])

    def prior(q):
        part = pl.ds(q * TILE, TILE)
        return pltpu.make_async_copy(halo_hbm.at[:, part], X.at[0:lead, part], insem.at[tiles + q])

    def place(i):
        if isinstance(i, int):
            return i // groups * TILE, i % groups * GROUP
        return pl.multiple_of(i // groups * TILE, TILE), lax.rem(i, groups) * GROUP

    def leaving(i, s):
        p, f = place(i)
        return pltpu.make_async_copy(F[s], feat_hbm.at[pl.ds(f, GROUP), pl.ds(p, TILE)], outsem.at[s])

    def product(i, s, m, n):
        p, f = place(i)
        count = ROWS // TILE
        acc = None
        for k in range(KT):
            rows = X[pl.ds(f + lead - k + m * count, count), pl.ds(p, TILE), :].reshape(ROWS, nchan)
            part = jnp.dot(rows, w[k, :, n : n + 256], preferred_element_type=F32)
            acc = part if acc is None else acc + part
        H[s][m * ROWS : (m + 1) * ROWS, n : n + 256] = acc

    def activate(i, s, g, r):
        p, f = place(i)
        at = g * TILE + r
        h = H[s][at : at + SUB, :]
        c = X[f + lead + g, pl.ds(p + r, SUB), :].astype(F32)
        value = c + (h + h * jnp.tanh(h))
        F[s][g, r : r + SUB, :] = value.astype(BF16)
        mean = jnp.sum(value * value, -1, keepdims=True) * (1.0 / nchan)
        R[at : at + SUB, :] = jnp.broadcast_to(lax.rsqrt(mean + 1e-06), (SUB, 128))

    def recur(i, s, r):
        p, f = place(i)
        rows = pl.ds(p + r, SUB)
        state = last[rows, :]
        for g in range(GROUP):
            scale = R[g * TILE + r : g * TILE + r + SUB, :]
            v = F[s][g, r : r + SUB, :].astype(F32)
            v = jnp.concatenate([v[:, n : n + 128] * scale for n in range(0, nchan, 128)], 1)
            state = state * kept[pl.ds(f + g, 1), :] + v
            pooled[window[f + g], rows, :] += state
        last[rows, :] = state

    products = [(m, n) for m in range(GROUP * TILE // ROWS) for n in range(0, nchan, 256)]

    def project(q):
        part = slice(q * TILE, (q + 1) * TILE)
        upper, lower = split(constants[0:nproj, :])
        both = jnp.concatenate([upper, lower], 0)
        for j in range(3):
            top, rest = split(pooled[j, part, :])
            value = times(both, top)
            sums[j * nproj : (j + 1) * nproj, part] = value[:nproj] + value[nproj:] + times(upper, rest)

    def stage(later, ls, i, s):
        work = [(g, r) for r in range(0, TILE, SUB) for g in range(GROUP)] + [(None, r) for r in range(0, TILE, SUB)]
        todo = [] if later is None else list(products)
        for at, (g, r) in enumerate(work):
            if todo and at * len(products) // len(work) >= len(products) - len(todo):
                product(later, ls, *todo.pop(0))
            if g is None:
                recur(i, s, r)
            else:
                activate(i, s, g, r)

    pieces = weights()
    for copy in pieces:
        copy.start()
    for q in range(tiles):
        prior(q).start()
        entering(q).start()
    kept[...] = constants[nproj : nproj + 1, :] * packing[:, 0:1]
    last[...] = jnp.zeros_like(last)
    pooled[...] = jnp.zeros_like(pooled)
    for copy in pieces:
        copy.wait()
    prior(0).wait()
    entering(0).wait()
    for m, n in products:
        product(0, 0, m, n)

    def body(step, _):
        i = 2 * step

        @pl.when(step > 0)
        def _():
            leaving(i - 2, 0).wait()
            leaving(i - 1, 1).wait()

        stage(i + 1, 1, i, 0)
        leaving(i, 0).start()
        q = (i + 2) // groups

        @pl.when(jnp.logical_and(lax.rem(i + 2, groups) == 0, q < tiles))
        def _():
            prior(q).wait()
            entering(q).wait()

        stage(i + 2, 0, i + 1, 1)
        leaving(i + 1, 1).start()
        return 0

    lax.fori_loop(0, total // 2 - 1, body, 0)
    leaving(total - 4, 0).wait()
    leaving(total - 3, 1).wait()
    stage(total - 1, 1, total - 2, 0)
    leaving(total - 2, 0).start()
    for q in range(tiles - 1):
        project(q)
    stage(None, None, total - 1, 1)
    leaving(total - 1, 1).start()
    project(tiles - 1)
    leaving(total - 2, 0).wait()
    leaving(total - 1, 1).wait()


def final_kernel(counts, *refs):
    per = counts.shape[0]
    latents = refs[-1]
    start = 0
    for index in range(len(refs) // 2):
        got, own = refs[2 * index], refs[2 * index + 1]
        ndev, rows, width = got.shape
        nproj = rows // per
        for i in range(per):
            part = slice(i * nproj, (i + 1) * nproj)
            total = own[part, :]
            for d in range(ndev):
                total = total + got[d, part, :].astype(F32)
            for n in range(0, width, 128):
                latents[i, :, start + n : start + n + 128] = total[:, n : n + 128] / counts[i : i + 1, :]
        start += width


def per_device(clips, w_time, gain, rate, keep, latent_ids, w_lat):
    _, nframe, npos, nchan = clips.shape
    nproj = w_lat.shape[1]
    ndev = lax.axis_size("tm")
    shards = lax.axis_size("dp")
    nall = nframe * ndev
    per = nframe // STRIDE
    me = lax.axis_index("tm")
    side = me % 2
    x = clips[0]

    half = w_time.shape[1] // 2
    mine = lax.dynamic_slice_in_dim(w_time, side * half, half, 1) * jnp.asarray(0.5, BF16)
    dc = rotated(mine, "dp", 2)
    da = rotated(mine, "dp", 1)
    db = rotated(mine, "dp", -1)
    so = swapped(mine, "tm")
    sa, sb, sc = swapped(da, "tm"), swapped(db, "tm"), swapped(dc, "tm")
    rate, gain, w_lat, _ = lax.optimization_barrier((rate, gain, w_lat, mine))
    halo = shifted(x[nframe - (KT - 1) :], "tm", 1)
    window = latent_ids - me.astype(jnp.int32) * per
    lane = jnp.arange(128, dtype=jnp.int32)[None]
    packing = jnp.where(lane < 64, keep[:, None], latent_ids.astype(F32)[:, None])
    local = jnp.broadcast_to(packing[None], (ndev, nframe, 128))
    packed = lax.all_to_all(local, "tm", 0, 0).reshape(nall, 128)

    inject = jnp.sqrt(-jnp.expm1(-2.0 * rate))
    row = jnp.arange(nproj + 8, dtype=jnp.int32)[:, None]
    padded = jnp.pad(w_lat.T.astype(F32), ((0, 8), (0, 0)))
    constants = jnp.where(row < nproj, padded * (inject * gain)[None], jnp.exp(-rate)[None])

    vmem = pl.BlockSpec(memory_space=pltpu.VMEM)
    smem = pl.BlockSpec(memory_space=pltpu.SMEM)
    hbm = pl.BlockSpec(memory_space=pltpu.HBM)

    stage_rows = GROUP * TILE
    conv = pl.pallas_call(
        functools.partial(conv_kernel, shards=shards),
        out_shape=(
            jax.ShapeDtypeStruct((nframe, npos, nchan), BF16),
            jax.ShapeDtypeStruct((npos, nchan), F32),
            jax.ShapeDtypeStruct((3 * nproj, npos), F32),
        ),
        in_specs=[smem, vmem] + [hbm] * 10 + [vmem],
        out_specs=(hbm, vmem, vmem),
        scratch_shapes=[
            pltpu.VMEM((KT, nchan, nchan), BF16),
            pltpu.VMEM((nframe + KT - 1, npos, nchan), BF16),
            pltpu.VMEM((stage_rows, nchan), F32),
            pltpu.VMEM((stage_rows, nchan), F32),
            pltpu.VMEM((GROUP, TILE, nchan), BF16),
            pltpu.VMEM((GROUP, TILE, nchan), BF16),
            pltpu.VMEM((stage_rows, 128), F32),
            pltpu.VMEM((3, npos, nchan), F32),
            pltpu.VMEM((nframe, nchan), F32),
            pltpu.SemaphoreType.DMA((8,)),
            pltpu.SemaphoreType.DMA((2 * npos // TILE,)),
            pltpu.SemaphoreType.DMA((2,)),
        ],
        compiler_params=pltpu.CompilerParams(vmem_limit_bytes=48 << 20),
        cost_estimate=pl.CostEstimate(
            flops=2 * KT * nframe * npos * nchan * nchan,
            bytes_accessed=4 * nframe * npos * nchan,
            transcendentals=nframe * npos * nchan,
        ),
        name="conv",
    )
    features, last, own = conv(window, packing, x, halo, mine, da, db, dc, so, sa, sb, sc, constants)
    packed, last = lax.optimization_barrier((packed, last))
    sends, counts = pl.pallas_call(
        spread_kernel,
        out_shape=(
            jax.ShapeDtypeStruct((ndev, per * nproj, npos), BF16),
            jax.ShapeDtypeStruct((per, 128), F32),
        ),
        in_specs=[vmem] * 5,
        out_specs=(vmem,) * 2,
        scratch_shapes=[pltpu.VMEM((nall, nchan), F32)],
        compiler_params=pltpu.CompilerParams(vmem_limit_bytes=16 << 20),
        name="spread",
    )(packed, rate[None], constants, last, own)
    outs = [lax.all_to_all(sends, "tm", 0, 0), own]
    latents = pl.pallas_call(
        final_kernel,
        out_shape=jax.ShapeDtypeStruct((per, nproj, npos), F32),
        in_specs=[vmem] * (1 + len(outs)),
        out_specs=vmem,
        compiler_params=pltpu.CompilerParams(vmem_limit_bytes=16 << 20),
        name="final",
    )(counts, *outs)
    return features[None], latents[None]


def solution(mesh):
    return jax.shard_map(
        per_device,
        mesh=mesh,
        in_specs=(P("dp", "tm", None, None), P(None, "dp", None), P(), P(), P("tm"), P("tm"), P()),
        out_specs=(P("dp", "tm", None, None), P("dp", "tm", None, None)),
        check_vma=False,
    )
```

profile of v0, /device:TPU:1, one launch (start us, length us, event | category | flops | bytes accessed | tf_op | source)
XLA Modules:
  0.0 83.4 jit_solution(1188297852906765751)
XLA Ops:
  0.6 1.0 %dynamic-slice_multiply_fusion.mine = bf16[3,64,512]{2,1,0:T(8,128)(2,1)S(1)} fusion(bf16[3,128,512]{2,1,0:T(8,128)(2,1)} %param.8, s32[]{:T(128)S(6)} %select_n.20), kind=kLoop, calls=%fused_computation.1 | loop fusion | flops 393216 | bytes 393220 | tf_op jit(solution)/shard_map/mul | solution.py:281
  1.6 2.1 %collective-permute-start.1 = (bf16[3,64,512]{2,1,0:T(8,128)(2,1)S(1)}, bf16[3,64,512]{2,1,0:T(8,128)(2,1)S(1)}, u32[]{:S(2)}, u32[]{:S(2)}) collective-permute-start(bf16[3,64,512]{2,1,0:T(8,128)(2,1)S(1)} %dynamic-slice_multiply_fusion.mine), channel_id=1, source_target_pairs={{0,32},{32,64},{64,96},{96,0},{1,33},{33,65},{65,97},{97,1},{2,34}... | collective-permute-start | bytes 589832 | tf_op jit(solution)/shard_map/ppermute | solution.py:23
  3.7 1.3 %collective-permute-start.2 = (bf16[3,64,512]{2,1,0:T(8,128)(2,1)S(1)}, bf16[3,64,512]{2,1,0:T(8,128)(2,1)S(1)}, u32[]{:S(2)}, u32[]{:S(2)}) collective-permute-start(bf16[3,64,512]{2,1,0:T(8,128)(2,1)S(1)} %dynamic-slice_multiply_fusion.mine), channel_id=1, source_target_pairs={{0,96},{32,0},{64,32},{96,64},{1,97},{33,1},{65,33},{97,65},{2,98}... | collective-permute-start | bytes 589832 | tf_op jit(solution)/shard_map/ppermute | solution.py:23
  5.1 1.6 %collective-permute-start.3 = (bf16[3,64,512]{2,1,0:T(8,128)(2,1)S(1)}, bf16[3,64,512]{2,1,0:T(8,128)(2,1)S(1)}, u32[]{:S(2)}, u32[]{:S(2)}) collective-permute-start(bf16[3,64,512]{2,1,0:T(8,128)(2,1)S(1)} %dynamic-slice_multiply_fusion.mine), channel_id=1, source_target_pairs={{0,64},{32,96},{64,0},{96,32},{1,65},{33,97},{65,1},{97,33},{2,66}... | collective-permute-start | bytes 589832 | tf_op jit(solution)/shard_map/ppermute | solution.py:23
  6.7 1.5 %collective-permute-start.4 = (bf16[3,64,512]{2,1,0:T(8,128)(2,1)S(1)}, bf16[3,64,512]{2,1,0:T(8,128)(2,1)S(1)}, u32[]{:S(2)}, u32[]{:S(2)}) collective-permute-start(bf16[3,64,512]{2,1,0:T(8,128)(2,1)S(1)} %dynamic-slice_multiply_fusion.mine), channel_id=1, source_target_pairs={{0,1},{1,0},{2,3},{3,2},{4,5},{5,4},{6,7},{7,6},{8,9},{9,8},{10,11... | collective-permute-start | bytes 589832 | tf_op jit(solution)/shard_map/ppermute | solution.py:32
  8.2 1.3 %slice_bitcast_fusion = bf16[2,512,512]{2,1,0:T(8,128)(2,1)S(1)} fusion(bf16[1,16,512,512]{3,2,1,0:T(8,128)(2,1)} %param.7), kind=kLoop, calls=%fused_computation | loop fusion | bytes 2097152 | tf_op jit(solution)/shard_map/slice | solution.py:288
  9.5 3.1 %collective-permute-start = (bf16[2,512,512]{2,1,0:T(8,128)(2,1)S(1)}, bf16[2,512,512]{2,1,0:T(8,128)(2,1)S(1)}, u32[]{:S(2)}, u32[]{:S(2)}) collective-permute-start(bf16[2,512,512]{2,1,0:T(8,128)(2,1)S(1)} %slice_bitcast_fusion), channel_id=1, source_target_pairs={{0,1},{1,2},{2,3},{3,4},{4,5},{5,6},{6,7},{7,8},{8,9},{9,10},{10,1... | collective-permute-start | bytes 3145736 | tf_op jit(solution)/shard_map/ppermute | solution.py:28
  12.6 0.7 fusion
  13.4 0.7 broadcast_select_fusion.packing
  14.1 0.7 broadcast_in_dim.67
  14.8 7.9 %all-to-all-start = ((f32[32,16,128]{2,1,0:T(8,128)}), f32[32,16,128]{2,1,0:T(8,128)S(1)}, u32[]{:S(2)}, u32[]{:S(2)}) async-start(f32[32,16,128]{2,1,0:T(8,128)} %broadcast_in_dim.67), calls=%async_computation | async-start | bytes 524288 | tf_op jit(solution)/shard_map/all_to_all | solution.py:293
  22.8 0.7 sqrt_multiply_fusion
  23.5 0.0 collective-permute-done.1.da
  23.5 0.3 collective-permute-start.5
  23.8 0.0 collective-permute-done.2.db
  23.8 0.3 collective-permute-start.6
  24.1 0.0 collective-permute-done.3.dc
  24.1 0.2 collective-permute-start.7
  24.3 0.8 multiply_select_fusion.constants
  25.1 0.0 collective-permute-done.4.so
  25.1 0.0 collective-permute-done.5.sa
  25.1 0.2 collective-permute-done.6.sb
  25.3 0.3 collective-permute-done.7.sc
  25.6 0.0 collective-permute-done.halo_hbm
  25.6 0.0 copy-start
  25.6 27.2 %conv.1 = (bf16[16,512,512]{2,1,0:T(8,128)(2,1)}, f32[512,512]{1,0:T(8,128)S(1)}, f32[48,512]{1,0:T(8,128)S(1)}) custom-call(s32[16]{0:T(128)S(1)} %get-tuple-element.25.window, f32[16,128]{1,0:T(8,128)S(1)} %broadcast_select_fusion.packing, bf16[16,512,512]{2,1,0:T(8,128)(2,1)} %bitcast.10, bf16[2,512,512]{2,1,0:T(8,128)(2,1)S(1)} %collective-permute-done.halo_hbm, ...), custom_call_target="tpu_custom_call" | custom-call | flops 12884901888 | bytes 16777216 | tf_op jit(solution)/shard_map/conv/pallas_call | solution.py:336
  52.8 0.0 all-to-all-done
  52.8 0.0 copy-done
  52.8 3.1 %spread.1 = (bf16[32,32,512]{2,1,0:T(8,128)(2,1)S(1)}, f32[2,128]{1,0:T(2,128)S(1)}) custom-call(f32[512,128]{1,0:T(8,128)S(1)} %bitcast.8, f32[1,512]{1,0:T(1,128)S(1)} %bitcast.9, f32[24,512]{1,0:T(8,128)S(1)} %multiply_select_fusion.constants, f32[512,512]{1,0:T(8,128)S(1)} %get-tuple-element.18.last, f32[48,512]{1,0:T(8,128)S(1)} %get-tuple-element.19.own.refs_1_), custom_call_target="tpu_custom_call" | custom-call | tf_op jit(solution)/shard_map/spread/pallas_call | solution.py:338
  55.9 26.7 %all_to_all.10.refs_0_ = bf16[32,32,512]{2,1,0:T(8,128)(2,1)S(1)} all-to-all(bf16[32,32,512]{2,1,0:T(8,128)(2,1)S(1)} %get-tuple-element.21), channel_id=1, replica_groups=mesh['dp'=4,'tm'=32] {'tm'}, dimensions={0} | all-to-all | bytes 2097152 | tf_op jit(solution)/shard_map/all_to_all | solution.py:350
  82.6 0.8 final.1
  (2 shorter events, 0.0 us)
Async XLA Ops:
  1.6 21.9 %collective-permute-start.1 = (bf16[3,64,512]{2,1,0:T(8,128)(2,1)S(1)}, bf16[3,64,512]{2,1,0:T(8,128)(2,1)S(1)}, u32[]{:S(2)}, u32[]{:S(2)}) collective-permute-start(bf16[3,64,512]{2,1,0:T(8,128)(2,1)S(1)} %dynamic-slice_multiply_fusion.mine), channel_id=1, source_target_pairs={{0,32},{32,64},{64,96},{96,0},{1,33},{33,65},{65,97},{97,1},{2,34}... | collective-permute-start | bytes 589832 | tf_op jit(solution)/shard_map/ppermute | solution.py:23
  3.7 20.1 %collective-permute-start.2 = (bf16[3,64,512]{2,1,0:T(8,128)(2,1)S(1)}, bf16[3,64,512]{2,1,0:T(8,128)(2,1)S(1)}, u32[]{:S(2)}, u32[]{:S(2)}) collective-permute-start(bf16[3,64,512]{2,1,0:T(8,128)(2,1)S(1)} %dynamic-slice_multiply_fusion.mine), channel_id=1, source_target_pairs={{0,96},{32,0},{64,32},{96,64},{1,97},{33,1},{65,33},{97,65},{2,98}... | collective-permute-start | bytes 589832 | tf_op jit(solution)/shard_map/ppermute | solution.py:23
  5.1 19.0 %collective-permute-start.3 = (bf16[3,64,512]{2,1,0:T(8,128)(2,1)S(1)}, bf16[3,64,512]{2,1,0:T(8,128)(2,1)S(1)}, u32[]{:S(2)}, u32[]{:S(2)}) collective-permute-start(bf16[3,64,512]{2,1,0:T(8,128)(2,1)S(1)} %dynamic-slice_multiply_fusion.mine), channel_id=1, source_target_pairs={{0,64},{32,96},{64,0},{96,32},{1,65},{33,97},{65,1},{97,33},{2,66}... | collective-permute-start | bytes 589832 | tf_op jit(solution)/shard_map/ppermute | solution.py:23
  6.7 18.4 %collective-permute-start.4 = (bf16[3,64,512]{2,1,0:T(8,128)(2,1)S(1)}, bf16[3,64,512]{2,1,0:T(8,128)(2,1)S(1)}, u32[]{:S(2)}, u32[]{:S(2)}) collective-permute-start(bf16[3,64,512]{2,1,0:T(8,128)(2,1)S(1)} %dynamic-slice_multiply_fusion.mine), channel_id=1, source_target_pairs={{0,1},{1,0},{2,3},{3,2},{4,5},{5,4},{6,7},{7,6},{8,9},{9,8},{10,11... | collective-permute-start | bytes 589832 | tf_op jit(solution)/shard_map/ppermute | solution.py:32
  9.5 16.1 %collective-permute-start = (bf16[2,512,512]{2,1,0:T(8,128)(2,1)S(1)}, bf16[2,512,512]{2,1,0:T(8,128)(2,1)S(1)}, u32[]{:S(2)}, u32[]{:S(2)}) collective-permute-start(bf16[2,512,512]{2,1,0:T(8,128)(2,1)S(1)} %slice_bitcast_fusion), channel_id=1, source_target_pairs={{0,1},{1,2},{2,3},{3,4},{4,5},{5,6},{6,7},{7,8},{8,9},{9,10},{10,1... | collective-permute-start | bytes 3145736 | tf_op jit(solution)/shard_map/ppermute | solution.py:28
  14.8 37.9 %all-to-all-start = ((f32[32,16,128]{2,1,0:T(8,128)}), f32[32,16,128]{2,1,0:T(8,128)S(1)}, u32[]{:S(2)}, u32[]{:S(2)}) async-start(f32[32,16,128]{2,1,0:T(8,128)} %broadcast_in_dim.67), calls=%async_computation | async-start | bytes 524288 | tf_op jit(solution)/shard_map/all_to_all | solution.py:293
  23.5 1.6 %collective-permute-start.5 = (bf16[3,64,512]{2,1,0:T(8,128)(2,1)S(1)}, bf16[3,64,512]{2,1,0:T(8,128)(2,1)S(1)}, u32[]{:S(2)}, u32[]{:S(2)}) collective-permute-start(bf16[3,64,512]{2,1,0:T(8,128)(2,1)S(1)} %collective-permute-done.1.da), channel_id=1, source_target_pairs={{0,1},{1,0},{2,3},{3,2},{4,5},{5,4},{6,7},{7,6},{8,9},{9,8},{10,11... | collective-permute-start | bytes 589832 | tf_op jit(solution)/shard_map/ppermute | solution.py:32
  23.8 1.5 %collective-permute-start.6 = (bf16[3,64,512]{2,1,0:T(8,128)(2,1)S(1)}, bf16[3,64,512]{2,1,0:T(8,128)(2,1)S(1)}, u32[]{:S(2)}, u32[]{:S(2)}) collective-permute-start(bf16[3,64,512]{2,1,0:T(8,128)(2,1)S(1)} %collective-permute-done.2.db), channel_id=1, source_target_pairs={{0,1},{1,0},{2,3},{3,2},{4,5},{5,4},{6,7},{7,6},{8,9},{9,8},{10,11... | collective-permute-start | bytes 589832 | tf_op jit(solution)/shard_map/ppermute | solution.py:32
  24.1 1.5 %collective-permute-start.7 = (bf16[3,64,512]{2,1,0:T(8,128)(2,1)S(1)}, bf16[3,64,512]{2,1,0:T(8,128)(2,1)S(1)}, u32[]{:S(2)}, u32[]{:S(2)}) collective-permute-start(bf16[3,64,512]{2,1,0:T(8,128)(2,1)S(1)} %collective-permute-done.3.dc), channel_id=1, source_target_pairs={{0,1},{1,0},{2,3},{3,2},{4,5},{5,4},{6,7},{7,6},{8,9},{9,8},{10,11... | collective-permute-start | bytes 589832 | tf_op jit(solution)/shard_map/ppermute | solution.py:32
  25.6 27.2 %copy-start = (f32[512]{0:T(512)S(1)}, f32[512]{0:T(512)}, u32[]{:S(2)}) copy-start(f32[512]{0:T(512)} %param.10) | copy-start | bytes 6148
where the time goes:
time: 83.8 us; the launch traced here: 83.4 us
  Pallas kernels  31.1 us (37%)
  blocking collectives  26.7 us (32%)
  starting transfers between devices  18.4 us (22%)
  other arithmetic  3.95 us (5%)
  local copies, waits for them, and re-layouts  2.02 us (2%)
    pallas_call x1, Pallas kernels, per_device(): conv(window, packing, x, halo, mine, da, db, dc, so, sa, sb, sc, constants)  27.2 us
    all_to_all x1, blocking collectives, per_device(): outs = [lax.all_to_all(sends, 'tm', 0, 0), own]  26.7 us
    all_to_all x1, starting transfers between devices, per_device(): packed = lax.all_to_all(local, 'tm', 0, 0).reshape(nall, 128)  7.92 us
    ppermute x3, starting transfers between devices, rotated(): lax.ppermute(value, axis, [(s, (s + steps) % count) for s in range(count)])  5.1 us
    pallas_call x1, Pallas kernels, per_device(): pl.pallas_call(spread_kernel, out_shape=(jax.ShapeDtypeStruct((ndev, per...  3.14 us
    ppermute x1, starting transfers between devices, shifted(): lax.ppermute(value, axis, [(s, s + steps) for s in range(count - steps)])  3.09 us
    ppermute x4, starting transfers between devices, swapped(): lax.ppermute(value, axis, [(s, s ^ 1) for s in range(lax.axis_size(axis))])  2.34 us
  transfers between devices with their start and end apart: 9, of which 2 were waited for; matrix products, arithmetic and copies ran while one was open for 6% of the time, Pallas kernels for 33%

commit v1 on v0

--- a/solution.py
+++ b/solution.py
@@ -88,8 +88,7 @@
     for r in range(0, nlat, group):
         value = jnp.concatenate([scaled * E[j : j + 1, :] for j in range(r, r + group)], 0)
         upper, lower = split(value)
-        z = times(jnp.concatenate([upper, lower], 0), top)
-        z = z[:rows] + z[rows:] + times(upper, rest)
+        z = times(upper, top) + times(upper, rest) + times(lower, top)
         first = r * nproj // per
         sends[first : first + rows // per] = z.reshape(rows // per, per, width).astype(BF16)
 
@@ -101,8 +100,8 @@
 
 
 def conv_kernel(
-    window, packing, x_hbm, halo_hbm, mine, da, db, dc, so, sa, sb, sc, constants,
-    feat_hbm, last, sums, w, X, HA, HB, FA, FB, R, pooled, kept, wsem, insem, outsem, *, shards,
+    window, local, x_hbm, halo_hbm, mine, da, db, dc, so, sa, sb, sc, constants,
+    feat_hbm, last, sums, w, X, HA, HB, FA, FB, R, pooled, kept, packing, wsem, insem, outsem, *, shards,
 ):
     nframe, npos, nchan = x_hbm.shape
     tiles, groups = npos // TILE, nframe // GROUP
@@ -197,17 +196,17 @@
             else:
                 activate(i, s, g, r)
 
-    pieces = weights()
+    pieces = weights() + [pltpu.make_async_copy(local.at[0], packing, wsem.at[8])]
     for copy in pieces:
         copy.start()
     for q in range(tiles):
         prior(q).start()
         entering(q).start()
-    kept[...] = constants[nproj : nproj + 1, :] * packing[:, 0:1]
     last[...] = jnp.zeros_like(last)
     pooled[...] = jnp.zeros_like(pooled)
     for copy in pieces:
         copy.wait()
+    kept[...] = constants[nproj : nproj + 1, :] * packing[:, 0:1]
     prior(0).wait()
     entering(0).wait()
     for m, n in products:
@@ -287,9 +286,9 @@
     rate, gain, w_lat, _ = lax.optimization_barrier((rate, gain, w_lat, mine))
     halo = shifted(x[nframe - (KT - 1) :], "tm", 1)
     window = latent_ids - me.astype(jnp.int32) * per
-    lane = jnp.arange(128, dtype=jnp.int32)[None]
-    packing = jnp.where(lane < 64, keep[:, None], latent_ids.astype(F32)[:, None])
-    local = jnp.broadcast_to(packing[None], (ndev, nframe, 128))
+    shape = (ndev, nframe, 128)
+    lane = lax.broadcasted_iota(jnp.int32, shape, 2) + jnp.minimum(lax.broadcasted_iota(jnp.int32, shape, 0), 0)
+    local = jnp.where(lane < 64, keep[None, :, None], latent_ids.astype(F32)[None, :, None])
     packed = lax.all_to_all(local, "tm", 0, 0).reshape(nall, 128)
 
     inject = jnp.sqrt(-jnp.expm1(-2.0 * rate))
@@ -309,7 +308,7 @@
             jax.ShapeDtypeStruct((npos, nchan), F32),
             jax.ShapeDtypeStruct((3 * nproj, npos), F32),
         ),
-        in_specs=[smem, vmem] + [hbm] * 10 + [vmem],
+        in_specs=[smem] + [hbm] * 11 + [vmem],
         out_specs=(hbm, vmem, vmem),
         scratch_shapes=[
             pltpu.VMEM((KT, nchan, nchan), BF16),
@@ -321,7 +320,8 @@
             pltpu.VMEM((stage_rows, 128), F32),
             pltpu.VMEM((3, npos, nchan), F32),
             pltpu.VMEM((nframe, nchan), F32),
-            pltpu.SemaphoreType.DMA((8,)),
+            pltpu.VMEM((nframe, 128), F32),
+            pltpu.SemaphoreType.DMA((9,)),
             pltpu.SemaphoreType.DMA((2 * npos // TILE,)),
             pltpu.SemaphoreType.DMA((2,)),
         ],
@@ -333,7 +333,7 @@
         ),
         name="conv",
     )
-    features, last, own = conv(window, packing, x, halo, mine, da, db, dc, so, sa, sb, sc, constants)
+    features, last, own = conv(window, local, x, halo, mine, da, db, dc, so, sa, sb, sc, constants)
     packed, last = lax.optimization_barrier((packed, last))
     sends, counts = pl.pallas_call(
         spread_kernel,

time: 83.8 us -> 83.8 us (level)
  no operation moved by 1% of the time
where the time goes in v1:
time: 83.8 us; the launch traced here: 83.4 us
  Pallas kernels  31.1 us (37%)
  blocking collectives  26.7 us (32%)
  starting transfers between devices  18.4 us (22%)
  other arithmetic  4.7 us (6%)
  local copies, waits for them, and re-layouts  1.3 us (2%)
    pallas_call x1, Pallas kernels, per_device(): conv(window, local, x, halo, mine, da, db, dc, so, sa, sb, sc, constants)  27.2 us
    all_to_all x1, blocking collectives, per_device(): outs = [lax.all_to_all(sends, 'tm', 0, 0), own]  26.7 us
    all_to_all x1, starting transfers between devices, per_device(): packed = lax.all_to_all(local, 'tm', 0, 0).reshape(nall, 128)  7.92 us
    ppermute x3, starting transfers between devices, rotated(): lax.ppermute(value, axis, [(s, (s + steps) % count) for s in range(count)])  5.1 us
    pallas_call x1, Pallas kernels, per_device(): pl.pallas_call(spread_kernel, out_shape=(jax.ShapeDtypeStruct((ndev, per...  3.1 us
    ppermute x1, starting transfers between devices, shifted(): lax.ppermute(value, axis, [(s, s + steps) for s in range(count - steps)])  3.09 us
    ppermute x4, starting transfers between devices, swapped(): lax.ppermute(value, axis, [(s, s ^ 1) for s in range(lax.axis_size(axis))])  2.34 us
  transfers between devices with their start and end apart: 9, of which 2 were waited for; matrix products, arithmetic and copies ran while one was open for 6% of the time, Pallas kernels for 33%

profile of v1, /device:TPU:1, one launch (start us, length us, event | category | flops | bytes accessed | tf_op | source)
XLA Modules:
  0.0 83.4 jit_solution(658319445427533776)
XLA Ops:
  0.6 1.0 %dynamic-slice_multiply_fusion.mine = bf16[3,64,512]{2,1,0:T(8,128)(2,1)S(1)} fusion(bf16[3,128,512]{2,1,0:T(8,128)(2,1)} %param.8, s32[]{:T(128)S(6)} %select_n.20), kind=kLoop, calls=%fused_computation.3 | loop fusion | flops 393216 | bytes 393220 | tf_op jit(solution)/shard_map/mul | solution.py:280
  1.6 2.1 %collective-permute-start.1 = (bf16[3,64,512]{2,1,0:T(8,128)(2,1)S(1)}, bf16[3,64,512]{2,1,0:T(8,128)(2,1)S(1)}, u32[]{:S(2)}, u32[]{:S(2)}) collective-permute-start(bf16[3,64,512]{2,1,0:T(8,128)(2,1)S(1)} %dynamic-slice_multiply_fusion.mine), channel_id=1, source_target_pairs={{0,32},{32,64},{64,96},{96,0},{1,33},{33,65},{65,97},{97,1},{2,34}... | collective-permute-start | bytes 589832 | tf_op jit(solution)/shard_map/ppermute | solution.py:23
  3.7 1.3 %collective-permute-start.2 = (bf16[3,64,512]{2,1,0:T(8,128)(2,1)S(1)}, bf16[3,64,512]{2,1,0:T(8,128)(2,1)S(1)}, u32[]{:S(2)}, u32[]{:S(2)}) collective-permute-start(bf16[3,64,512]{2,1,0:T(8,128)(2,1)S(1)} %dynamic-slice_multiply_fusion.mine), channel_id=1, source_target_pairs={{0,96},{32,0},{64,32},{96,64},{1,97},{33,1},{65,33},{97,65},{2,98}... | collective-permute-start | bytes 589832 | tf_op jit(solution)/shard_map/ppermute | solution.py:23
  5.1 1.6 %collective-permute-start.3 = (bf16[3,64,512]{2,1,0:T(8,128)(2,1)S(1)}, bf16[3,64,512]{2,1,0:T(8,128)(2,1)S(1)}, u32[]{:S(2)}, u32[]{:S(2)}) collective-permute-start(bf16[3,64,512]{2,1,0:T(8,128)(2,1)S(1)} %dynamic-slice_multiply_fusion.mine), channel_id=1, source_target_pairs={{0,64},{32,96},{64,0},{96,32},{1,65},{33,97},{65,1},{97,33},{2,66}... | collective-permute-start | bytes 589832 | tf_op jit(solution)/shard_map/ppermute | solution.py:23
  6.7 1.5 %collective-permute-start.4 = (bf16[3,64,512]{2,1,0:T(8,128)(2,1)S(1)}, bf16[3,64,512]{2,1,0:T(8,128)(2,1)S(1)}, u32[]{:S(2)}, u32[]{:S(2)}) collective-permute-start(bf16[3,64,512]{2,1,0:T(8,128)(2,1)S(1)} %dynamic-slice_multiply_fusion.mine), channel_id=1, source_target_pairs={{0,1},{1,0},{2,3},{3,2},{4,5},{5,4},{6,7},{7,6},{8,9},{9,8},{10,11... | collective-permute-start | bytes 589832 | tf_op jit(solution)/shard_map/ppermute | solution.py:32
  8.2 1.3 %slice_bitcast_fusion = bf16[2,512,512]{2,1,0:T(8,128)(2,1)S(1)} fusion(bf16[1,16,512,512]{3,2,1,0:T(8,128)(2,1)} %param.7), kind=kLoop, calls=%fused_computation | loop fusion | bytes 2097152 | tf_op jit(solution)/shard_map/slice | solution.py:287
  9.5 3.1 %collective-permute-start = (bf16[2,512,512]{2,1,0:T(8,128)(2,1)S(1)}, bf16[2,512,512]{2,1,0:T(8,128)(2,1)S(1)}, u32[]{:S(2)}, u32[]{:S(2)}) collective-permute-start(bf16[2,512,512]{2,1,0:T(8,128)(2,1)S(1)} %slice_bitcast_fusion), channel_id=1, source_target_pairs={{0,1},{1,2},{2,3},{3,4},{4,5},{5,6},{6,7},{7,8},{8,9},{9,10},{10,1... | collective-permute-start | bytes 3145736 | tf_op jit(solution)/shard_map/ppermute | solution.py:28
  12.6 0.7 fusion.1
  13.4 1.5 %fusion.local = f32[32,16,128]{2,1,0:T(8,128)} fusion(f32[16]{0:T(128)S(1)} %get-tuple-element.24, f32[16]{0:T(128)} %param.11, s32[32]{0:T(128)S(1)} %iota_minimum_fusion), kind=kLoop, calls=%fused_computation.2 | loop fusion | flops 196608 | bytes 262400 | tf_op jit(solution)/shard_map/jit(_where)/select_n | solution.py:291
  14.9 7.9 %all-to-all-start = ((f32[32,16,128]{2,1,0:T(8,128)}), f32[32,16,128]{2,1,0:T(8,128)S(1)}, u32[]{:S(2)}, u32[]{:S(2)}) async-start(f32[32,16,128]{2,1,0:T(8,128)} %fusion.local), calls=%async_computation | async-start | bytes 524288 | tf_op jit(solution)/shard_map/all_to_all | solution.py:292
  22.8 0.7 sqrt_multiply_fusion
  23.5 0.0 collective-permute-done.1.da
  23.5 0.3 collective-permute-start.5
  23.8 0.0 collective-permute-done.2.db
  23.8 0.3 collective-permute-start.6
  24.1 0.0 collective-permute-done.3.dc
  24.1 0.2 collective-permute-start.7
  24.4 0.8 multiply_select_fusion.constants
  25.1 0.0 collective-permute-done.4.so
  25.1 0.0 collective-permute-done.5.sa
  25.2 0.2 collective-permute-done.6.sb
  25.3 0.3 collective-permute-done.7.sc
  25.6 0.0 collective-permute-done.halo_hbm
  25.6 0.0 copy-start
  25.6 27.2 %conv.1 = (bf16[16,512,512]{2,1,0:T(8,128)(2,1)}, f32[512,512]{1,0:T(8,128)S(1)}, f32[48,512]{1,0:T(8,128)S(1)}) custom-call(s32[16]{0:T(128)S(1)} %get-tuple-element.25.window, f32[32,16,128]{2,1,0:T(8,128)} %fusion.local, bf16[16,512,512]{2,1,0:T(8,128)(2,1)} %bitcast.10, bf16[2,512,512]{2,1,0:T(8,128)(2,1)S(1)} %collective-permute-done.halo_hbm, ...), custom_call_target="tpu_custom_call" | custom-call | flops 12884901888 | bytes 16777216 | tf_op jit(solution)/shard_map/conv/pallas_call | solution.py:336
  52.8 0.0 all-to-all-done
  52.8 0.0 copy-done
  52.8 3.1 %spread.1 = (bf16[32,32,512]{2,1,0:T(8,128)(2,1)S(1)}, f32[2,128]{1,0:T(2,128)S(1)}) custom-call(f32[512,128]{1,0:T(8,128)S(1)} %bitcast.8, f32[1,512]{1,0:T(1,128)S(1)} %bitcast.9, f32[24,512]{1,0:T(8,128)S(1)} %multiply_select_fusion.constants, f32[512,512]{1,0:T(8,128)S(1)} %get-tuple-element.18.last, f32[48,512]{1,0:T(8,128)S(1)} %get-tuple-element.19.own.refs_1_), custom_call_target="tpu_custom_call" | custom-call | tf_op jit(solution)/shard_map/spread/pallas_call | solution.py:338
  55.9 26.7 %all_to_all.10.refs_0_ = bf16[32,32,512]{2,1,0:T(8,128)(2,1)S(1)} all-to-all(bf16[32,32,512]{2,1,0:T(8,128)(2,1)S(1)} %get-tuple-element.21), channel_id=1, replica_groups=mesh['dp'=4,'tm'=32] {'tm'}, dimensions={0} | all-to-all | bytes 2097152 | tf_op jit(solution)/shard_map/all_to_all | solution.py:350
  82.6 0.8 final.1
  (2 shorter events, 0.0 us)
Async XLA Ops:
  1.6 21.9 %collective-permute-start.1 = (bf16[3,64,512]{2,1,0:T(8,128)(2,1)S(1)}, bf16[3,64,512]{2,1,0:T(8,128)(2,1)S(1)}, u32[]{:S(2)}, u32[]{:S(2)}) collective-permute-start(bf16[3,64,512]{2,1,0:T(8,128)(2,1)S(1)} %dynamic-slice_multiply_fusion.mine), channel_id=1, source_target_pairs={{0,32},{32,64},{64,96},{96,0},{1,33},{33,65},{65,97},{97,1},{2,34}... | collective-permute-start | bytes 589832 | tf_op jit(solution)/shard_map/ppermute | solution.py:23
  3.7 20.1 %collective-permute-start.2 = (bf16[3,64,512]{2,1,0:T(8,128)(2,1)S(1)}, bf16[3,64,512]{2,1,0:T(8,128)(2,1)S(1)}, u32[]{:S(2)}, u32[]{:S(2)}) collective-permute-start(bf16[3,64,512]{2,1,0:T(8,128)(2,1)S(1)} %dynamic-slice_multiply_fusion.mine), channel_id=1, source_target_pairs={{0,96},{32,0},{64,32},{96,64},{1,97},{33,1},{65,33},{97,65},{2,98}... | collective-permute-start | bytes 589832 | tf_op jit(solution)/shard_map/ppermute | solution.py:23
  5.1 19.1 %collective-permute-start.3 = (bf16[3,64,512]{2,1,0:T(8,128)(2,1)S(1)}, bf16[3,64,512]{2,1,0:T(8,128)(2,1)S(1)}, u32[]{:S(2)}, u32[]{:S(2)}) collective-permute-start(bf16[3,64,512]{2,1,0:T(8,128)(2,1)S(1)} %dynamic-slice_multiply_fusion.mine), channel_id=1, source_target_pairs={{0,64},{32,96},{64,0},{96,32},{1,65},{33,97},{65,1},{97,33},{2,66}... | collective-permute-start | bytes 589832 | tf_op jit(solution)/shard_map/ppermute | solution.py:23
  6.7 18.4 %collective-permute-start.4 = (bf16[3,64,512]{2,1,0:T(8,128)(2,1)S(1)}, bf16[3,64,512]{2,1,0:T(8,128)(2,1)S(1)}, u32[]{:S(2)}, u32[]{:S(2)}) collective-permute-start(bf16[3,64,512]{2,1,0:T(8,128)(2,1)S(1)} %dynamic-slice_multiply_fusion.mine), channel_id=1, source_target_pairs={{0,1},{1,0},{2,3},{3,2},{4,5},{5,4},{6,7},{7,6},{8,9},{9,8},{10,11... | collective-permute-start | bytes 589832 | tf_op jit(solution)/shard_map/ppermute | solution.py:32
  9.5 16.1 %collective-permute-start = (bf16[2,512,512]{2,1,0:T(8,128)(2,1)S(1)}, bf16[2,512,512]{2,1,0:T(8,128)(2,1)S(1)}, u32[]{:S(2)}, u32[]{:S(2)}) collective-permute-start(bf16[2,512,512]{2,1,0:T(8,128)(2,1)S(1)} %slice_bitcast_fusion), channel_id=1, source_target_pairs={{0,1},{1,2},{2,3},{3,4},{4,5},{5,6},{6,7},{7,8},{8,9},{9,10},{10,1... | collective-permute-start | bytes 3145736 | tf_op jit(solution)/shard_map/ppermute | solution.py:28
  14.9 37.9 %all-to-all-start = ((f32[32,16,128]{2,1,0:T(8,128)}), f32[32,16,128]{2,1,0:T(8,128)S(1)}, u32[]{:S(2)}, u32[]{:S(2)}) async-start(f32[32,16,128]{2,1,0:T(8,128)} %fusion.local), calls=%async_computation | async-start | bytes 524288 | tf_op jit(solution)/shard_map/all_to_all | solution.py:292
  23.5 1.6 %collective-permute-start.5 = (bf16[3,64,512]{2,1,0:T(8,128)(2,1)S(1)}, bf16[3,64,512]{2,1,0:T(8,128)(2,1)S(1)}, u32[]{:S(2)}, u32[]{:S(2)}) collective-permute-start(bf16[3,64,512]{2,1,0:T(8,128)(2,1)S(1)} %collective-permute-done.1.da), channel_id=1, source_target_pairs={{0,1},{1,0},{2,3},{3,2},{4,5},{5,4},{6,7},{7,6},{8,9},{9,8},{10,11... | collective-permute-start | bytes 589832 | tf_op jit(solution)/shard_map/ppermute | solution.py:32
  23.8 1.5 %collective-permute-start.6 = (bf16[3,64,512]{2,1,0:T(8,128)(2,1)S(1)}, bf16[3,64,512]{2,1,0:T(8,128)(2,1)S(1)}, u32[]{:S(2)}, u32[]{:S(2)}) collective-permute-start(bf16[3,64,512]{2,1,0:T(8,128)(2,1)S(1)} %collective-permute-done.2.db), channel_id=1, source_target_pairs={{0,1},{1,0},{2,3},{3,2},{4,5},{5,4},{6,7},{7,6},{8,9},{9,8},{10,11... | collective-permute-start | bytes 589832 | tf_op jit(solution)/shard_map/ppermute | solution.py:32
  24.1 1.5 %collective-permute-start.7 = (bf16[3,64,512]{2,1,0:T(8,128)(2,1)S(1)}, bf16[3,64,512]{2,1,0:T(8,128)(2,1)S(1)}, u32[]{:S(2)}, u32[]{:S(2)}) collective-permute-start(bf16[3,64,512]{2,1,0:T(8,128)(2,1)S(1)} %collective-permute-done.3.dc), channel_id=1, source_target_pairs={{0,1},{1,0},{2,3},{3,2},{4,5},{5,4},{6,7},{7,6},{8,9},{9,8},{10,11... | collective-permute-start | bytes 589832 | tf_op jit(solution)/shard_map/ppermute | solution.py:32
  25.6 27.2 %copy-start = (f32[512]{0:T(512)S(1)}, f32[512]{0:T(512)}, u32[]{:S(2)}) copy-start(f32[512]{0:T(512)} %param.10) | copy-start | bytes 6148
